TPU v7x, 1024 devices: a whole 4x8x16 slice. The times are simulated.
1024 devices in a mesh: dp: 32 (over z, core), ctx: 16 (over y_lo, x), chan: 2 (over y_hi).
Axes of the slice: x: 4, y: 8 (y_hi: 2, y_lo: 4; y = y_hi * 4 + y_lo), z: 16, core: 2. Of those that a mesh axis runs over, the one named last changes fastest.
Arguments:
- layer_input: bfloat16 [4096, 16384], P(('dp', 'chan'), 'ctx'), may hold values from -6 to 6
- grad_output: bfloat16 [4096, 16384], P(('dp', 'chan'), 'ctx'), may hold values from -6 to 6
- filter_taps: float32 [64, 64, 16384], P(('dp', 'chan'), 'ctx'), may hold values from -2 to 2
Outputs:
- grad_input: bfloat16 [4096, 16384], P(('dp', 'chan'), 'ctx')
- grad_filter: float32 [64, 64, 16384], P(('dp', 'chan'), 'ctx')
All inputs are finite; a program needn't handle non-finite values.
Results may differ from a plain program's by a relative error of at most 0.001.
Values may be sent and summed in bfloat16 or wider, within the bound.
A program may use at most 32 MiB of HBM per device.

v0:
```python
import math

import jax
import jax.numpy as jnp
from jax import lax
from jax.sharding import PartitionSpec as P


def angle_table(count_rows, count_cols, modulus):
    row_index = lax.broadcasted_iota(jnp.int32, (count_rows, count_cols), 0)
    col_index = lax.broadcasted_iota(jnp.int32, (count_rows, count_cols), 1)
    phase_index = row_index * col_index % modulus
    radians = phase_index.astype(jnp.float32) * (2.0 * math.pi / modulus)
    return (jnp.cos(radians), jnp.sin(radians))


def product(pattern, left_operand, right_operand):
    return jnp.einsum(
        pattern,
        left_operand,
        right_operand,
        precision=lax.Precision.HIGHEST,
        preferred_element_type=jnp.float32,
    )


def forward(signal, tables):
    (cos_one, sin_one), (cos_turn, sin_turn), (cos_two, sin_two) = tables
    real_first = product("kn,cnm->ckm", cos_one, signal)
    imag_first = -product("kn,cnm->ckm", sin_one, signal)
    real_turned = real_first * cos_turn + imag_first * sin_turn
    imag_turned = imag_first * cos_turn - real_first * sin_turn
    real_out = product("ckm,mj->ckj", real_turned, cos_two) + product(
        "ckm,mj->ckj", imag_turned, sin_two
    )
    imag_out = product("ckm,mj->ckj", imag_turned, cos_two) - product(
        "ckm,mj->ckj", real_turned, sin_two
    )
    return (real_out, imag_out)


def inverse(real_spec, imag_spec, tables):
    (cos_one, sin_one), (cos_turn, sin_turn), (cos_two, sin_two) = tables
    real_first = product("ckj,mj->ckm", real_spec, cos_two) - product(
        "ckj,mj->ckm", imag_spec, sin_two
    )
    imag_first = product("ckj,mj->ckm", real_spec, sin_two) + product(
        "ckj,mj->ckm", imag_spec, cos_two
    )
    real_turned = real_first * cos_turn - imag_first * sin_turn
    imag_turned = real_first * sin_turn + imag_first * cos_turn
    signal = product("kn,ckm->cnm", cos_one, real_turned) - product(
        "kn,ckm->cnm", sin_one, imag_turned
    )
    return signal / (cos_one.shape[0] * cos_two.shape[0])


def shards(layer_input, grad_output, filter_taps):
    ctx_count = lax.axis_size("ctx")
    pencil = layer_input.shape[0] // ctx_count
    length = layer_input.shape[1] * ctx_count
    inner_size = min(128, length // 2)
    outer_size = 2 * length // inner_size
    half_outer = outer_size // 2
    tables = (
        angle_table(outer_size, half_outer, outer_size),
        angle_table(outer_size, inner_size, outer_size * inner_size),
        angle_table(inner_size, inner_size, inner_size),
    )
    block_shape = (pencil, half_outer, inner_size)
    filter_real, filter_imag = forward(filter_taps.reshape(block_shape), tables)
    moved_input, moved_grad = (
        lax.all_to_all(layer_input, "ctx", split_axis=0, concat_axis=1, tiled=True),
        lax.all_to_all(grad_output, "ctx", split_axis=0, concat_axis=1, tiled=True),
    )
    grad_real, grad_imag = forward(moved_grad.reshape(block_shape).astype(jnp.float32), tables)
    back_real = filter_real * grad_real + filter_imag * grad_imag
    back_imag = filter_real * grad_imag - filter_imag * grad_real
    local_back = inverse(back_real, back_imag, tables).reshape(pencil, length).astype(jnp.bfloat16)
    grad_input = lax.all_to_all(local_back, "ctx", split_axis=1, concat_axis=0, tiled=True)
    input_real, input_imag = forward(moved_input.reshape(block_shape).astype(jnp.float32), tables)
    tap_real = grad_real * input_real + grad_imag * input_imag
    tap_imag = grad_imag * input_real - grad_real * input_imag
    grad_scale = 1.0 / math.sqrt(length)
    local_taps = inverse(tap_real, tap_imag, tables) * grad_scale
    return (grad_input, local_taps.reshape(1, pencil, length))


def solution(mesh):
    in_specs = (P(("dp", "chan"), "ctx"), P(("dp", "chan"), "ctx"), P(("dp", "chan"), "ctx", None))
    out_specs = (P(("dp", "chan"), "ctx"), P(("dp", "chan"), "ctx", None))
    return jax.shard_map(shards, mesh=mesh, in_specs=in_specs, out_specs=out_specs, check_vma=False)
```

profile of v0, /device:TPU:2, one launch (start us, length us, event | category | flops | bytes accessed | tf_op | source)
XLA Modules:
  0.0 73.1 jit_solution(14695759556675631394)
XLA Ops:
  0.6 1.6 %all_to_all.36 = bf16[16,4,1024]{2,1,0:T(4,128)(2,1)} reshape(bf16[64,1024]{1,0:T(8,128)(2,1)} %param.4) | data formatting | bytes 262144 | tf_op jit(solution)/shard_map/all_to_all | solution.py:74
  2.2 16.6 %all-to-all-start = ((bf16[16,4,1024]{2,1,0:T(4,128)(2,1)}), bf16[16,4,1024]{2,1,0:T(4,128)(2,1)S(1)}, u32[]{:S(2)}, u32[]{:S(2)}) async-start(bf16[16,4,1024]{2,1,0:T(4,128)(2,1)} %all_to_all.36), calls=%async_computation | async-start | bytes 262144 | tf_op jit(solution)/shard_map/all_to_all | solution.py:74
  19.4 1.1 %convolution_negate_fusion.2 = f32[256,4,128]{2,0,1:T(8,128)S(1)} fusion(f32[1,4,128,128]{3,1,2,0:T(4,128)S(1)} %bitcast.124), kind=kOutput, calls=%fused_computation.2 | convolution fusion | flops 201916416 | bytes 786432 | tf_op jit(solution)/shard_map/kn,cnm->ckm/dot_general | solution.py:18
  20.5 1.1 %fusion.38 = f32[256,4,128]{2,0,1:T(8,128)S(1)} fusion(f32[1,4,128,128]{3,1,2,0:T(4,128)S(1)} %bitcast.125), kind=kOutput, calls=%fused_computation.63 | convolution fusion | flops 201785344 | bytes 786432 | tf_op jit(solution)/shard_map/kn,cnm->ckm/dot_general | solution.py:18
  21.5 0.8 %fusion.17 = f32[4,256,128]{2,1,0:T(8,128)S(1)} fusion(f32[256,4,128]{2,0,1:T(8,128)S(1)} %fusion.38, f32[256,4,128]{2,0,1:T(8,128)S(1)} %convolution_negate_fusion.2, f32[256,128]{1,0:T(8,128)S(1)} %get-tuple-element.8, f32[256,128]{1,0:T(8,128)S(1)} %get-tuple-element.9), kind=kOutput, calls=%fused_computation.32 | convolution fusion | flops 201949184 | bytes 1835008 | tf_op jit(solution)/shard_map/ckm,mj->ckj/dot_general | solution.py:18
  24.0 0.8 %convolution_subtract_fusion.4 = f32[4,256,128]{2,1,0:T(8,128)S(1)} fusion(f32[4,256,128]{2,1,0:T(8,128)S(1)} %fusion.17, f32[256,4,128]{2,0,1:T(8,128)S(1)} %convolution_negate_fusion.2, f32[256,4,128]{2,0,1:T(8,128)S(1)} %fusion.38, f32[256,128]{1,0:T(8,128)S(1)} %get-tuple-element.8, f32[256,128]{1,0:T(8,128)S(1)} %get-tuple-element.9), kind=kOutput, calls=%fused_computation.10 | convolution fusion | flops 202080256 | bytes 2359296 | tf_op jit(solution)/shard_map/ckm,mj->ckj/dot_general | solution.py:18
  24.8 0.8 %convolution_add_fusion.4 = f32[4,256,128]{2,1,0:T(8,128)S(1)} fusion(f32[4,256,128]{2,1,0:T(8,128)S(1)} %fusion.21, f32[256,4,128]{2,0,1:T(8,128)S(1)} %fusion.38, f32[256,4,128]{2,0,1:T(8,128)S(1)} %convolution_negate_fusion.2, f32[256,128]{1,0:T(8,128)S(1)} %get-tuple-element.8, f32[256,128]{1,0:T(8,128)S(1)} %get-tuple-element.9), kind=kOutput, calls=%fused_computation.12 | convolution fusion | flops 202080256 | bytes 2359296 | tf_op jit(solution)/shard_map/ckm,mj->ckj/dot_general | solution.py:18
  25.6 1.0 %all-to-all-done = bf16[16,4,1024]{2,1,0:T(4,128)(2,1)S(1)} async-done(((bf16[16,4,1024]{2,1,0:T(4,128)(2,1)}), bf16[16,4,1024]{2,1,0:T(4,128)(2,1)S(1)}, u32[]{:S(2)}, u32[]{:S(2)}) %all-to-all-start) | async-done | bytes 131104 | tf_op jit(solution)/shard_map/all_to_all | solution.py:74
  26.6 6.6 %all-to-all-start.2 = ((bf16[16,4,1024]{2,1,0:T(4,128)(2,1)}), bf16[16,4,1024]{2,1,0:T(4,128)(2,1)S(1)}, u32[]{:S(2)}, u32[]{:S(2)}) async-start(bf16[16,4,1024]{2,1,0:T(4,128)(2,1)} %all_to_all.42), calls=%async_computation.2 | async-start | bytes 262144 | tf_op jit(solution)/shard_map/all_to_all | solution.py:73
  35.0 5.8 %all-to-all-done.2 = bf16[16,4,1024]{2,1,0:T(4,128)(2,1)S(1)} async-done(((bf16[16,4,1024]{2,1,0:T(4,128)(2,1)}), bf16[16,4,1024]{2,1,0:T(4,128)(2,1)S(1)}, u32[]{:S(2)}, u32[]{:S(2)}) %all-to-all-start.2) | async-done | bytes 131104 | tf_op jit(solution)/shard_map/all_to_all | solution.py:73
  42.6 0.8 %fusion.5 = f32[4,256,128]{2,1,0:T(8,128)S(1)} fusion(f32[256,4,128]{2,0,1:T(8,128)S(1)} %fusion.60, f32[256,4,128]{2,0,1:T(8,128)S(1)} %convolution_negate_fusion, f32[256,128]{1,0:T(8,128)S(1)} %get-tuple-element.8, f32[256,128]{1,0:T(8,128)S(1)} %get-tuple-element.9), kind=kOutput, calls=%fused_computation.20 | convolution fusion | flops 201949184 | bytes 1835008 | tf_op jit(solution)/shard_map/ckm,mj->ckj/dot_general | solution.py:18
  45.9 0.8 %convolution_subtract_fusion.1 = f32[4,256,128]{2,1,0:T(8,128)S(1)} fusion(f32[4,256,128]{2,1,0:T(8,128)S(1)} %fusion.5, f32[256,4,128]{2,0,1:T(8,128)S(1)} %convolution_negate_fusion, f32[256,4,128]{2,0,1:T(8,128)S(1)} %fusion.60, f32[256,128]{1,0:T(8,128)S(1)} %get-tuple-element.8, f32[256,128]{1,0:T(8,128)S(1)} %get-tuple-element.9), kind=kOutput, calls=%fused_computation.5 | convolution fusion | flops 202080256 | bytes 2359296 | tf_op jit(solution)/shard_map/ckm,mj->ckj/dot_general | solution.py:18
  46.7 0.8 %convolution_add_fusion.1 = f32[4,256,128]{2,1,0:T(8,128)S(1)} fusion(f32[4,256,128]{2,1,0:T(8,128)S(1)} %fusion.9, f32[256,4,128]{2,0,1:T(8,128)S(1)} %fusion.60, f32[256,4,128]{2,0,1:T(8,128)S(1)} %convolution_negate_fusion, f32[256,128]{1,0:T(8,128)S(1)} %get-tuple-element.8, f32[256,128]{1,0:T(8,128)S(1)} %get-tuple-element.9), kind=kOutput, calls=%fused_computation.6 | convolution fusion | flops 202080256 | bytes 2359296 | tf_op jit(solution)/shard_map/ckm,mj->ckj/dot_general | solution.py:18
  47.5 0.8 %convolution_subtract_fusion.3 = f32[4,256,128]{2,1,0:T(8,128)S(1)} fusion(f32[4,256,128]{2,1,0:T(8,128)S(1)} %fusion.11, f32[256,4,128]{2,0,1:T(8,128)S(1)} %convolution_negate_fusion.1, f32[256,4,128]{2,0,1:T(8,128)S(1)} %fusion.63, f32[256,128]{1,0:T(8,128)S(1)} %get-tuple-element.8, f32[256,128]{1,0:T(8,128)S(1)} %get-tuple-element.9), kind=kOutput, calls=%fused_computation.9 | convolution fusion | flops 202080256 | bytes 2359296 | tf_op jit(solution)/shard_map/ckm,mj->ckj/dot_general | solution.py:18
  48.4 1.1 %multiply_subtract_fusion = (f32[4,256,128]{2,1,0:T(8,128)S(1)}, f32[4,256,128]{2,1,0:T(8,128)S(1)}, f32[4,256,128]{2,1,0:T(8,128)S(1)}, f32[4,256,128]{2,1,0:T(8,128)S(1)}) fusion(f32[4,256,128]{2,1,0:T(8,128)S(1)} %convolution_subtract_fusion.1, f32[4,256,128]{2,1,0:T(8,128)S(1)} %convolution_subtract_fusion.3, ...), kind=kOutput, calls=%fused_computation.45 | convolution fusion | flops 203653120 | bytes 6553600 | tf_op jit(solution)/shard_map/ckm,mj->ckj/dot_general | solution.py:18
  49.4 0.8 %fusion.76 = f32[4,256,128]{2,1,0:T(8,128)S(1)} fusion(f32[4,256,128]{2,1,0:T(8,128)S(1)} %get-tuple-element.3), kind=kOutput, calls=%fused_computation.110 | convolution fusion | flops 201555968 | bytes 1048576 | tf_op jit(solution)/shard_map/ckj,mj->ckm/dot_general | solution.py:18
  51.1 1.0 %fusion.81 = f32[4,256,128]{2,1,0:T(8,128)S(1)} fusion(f32[4,256,128]{2,1,0:T(8,128)S(1)} %get-tuple-element.6), kind=kOutput, calls=%fused_computation.115 | convolution fusion | flops 201555968 | bytes 1048576 | tf_op jit(solution)/shard_map/ckj,mj->ckm/dot_general | solution.py:18
  53.8 0.8 %convolution_subtract_fusion = f32[4,256,128]{2,1,0:T(8,128)S(1)} fusion(f32[4,256,128]{2,1,0:T(8,128)S(1)} %fusion.89, f32[4,256,128]{2,1,0:T(8,128)S(1)} %get-tuple-element.2), kind=kOutput, calls=%fused_computation.4 | convolution fusion | flops 201687040 | bytes 1572864 | tf_op jit(solution)/shard_map/ckj,mj->ckm/dot_general | solution.py:18
  56.3 1.4 %fusion.33 = f32[4,128,128]{2,1,0:T(8,128)S(1)} fusion(f32[4,256,128]{2,1,0:T(8,128)S(1)} %convolution_add_fusion.2, f32[4,256,128]{2,1,0:T(8,128)S(1)} %convolution_subtract_fusion.2, f32[256,128]{1,0:T(8,128)S(1)} %get-tuple-element.8, f32[256,128]{1,0:T(8,128)S(1)} %get-tuple-element.9), kind=kOutput, calls=%fused_computation.52 | convolution fusion | flops 202178560 | bytes 1572864 | tf_op jit(solution)/shard_map/kn,ckm->cnm/dot_general | solution.py:18
  57.7 1.4 %fusion.4 = bf16[4,128,128]{1,2,0:T(8,128)(2,1)S(1)} fusion(f32[4,128,128]{2,1,0:T(8,128)S(1)} %fusion.33, f32[4,256,128]{2,1,0:T(8,128)S(1)} %convolution_add_fusion.2, f32[4,256,128]{2,1,0:T(8,128)S(1)} %convolution_subtract_fusion.2, f32[256,128]{1,0:T(8,128)S(1)} %get-tuple-element.8, f32[256,128]{1,0:T(8,128)S(1)} %get-tuple-element.9), kind=kOutput, calls=%fused_computation.19 | convolution fusion | flops 202375168 | bytes 1703936 | tf_op jit(solution)/shard_map/kn,ckm->cnm/dot_general | solution.py:18
  60.0 4.8 %all-to-all-start.1 = ((bf16[4,16,1024]{2,0,1:T(4,128)(2,1)}), bf16[4,16,1024]{2,0,1:T(4,128)(2,1)S(1)}, u32[]{:S(2)}, u32[]{:S(2)}) async-start(bf16[4,16,1024]{2,0,1:T(4,128)(2,1)} %copy.32), calls=%async_computation.1 | async-start | bytes 262144 | tf_op jit(solution)/shard_map/all_to_all | solution.py:80
  64.8 1.4 %fusion.26 = f32[4,128,128]{2,1,0:T(8,128)S(1)} fusion(f32[4,256,128]{2,1,0:T(8,128)S(1)} %convolution_add_fusion, f32[4,256,128]{2,1,0:T(8,128)S(1)} %convolution_subtract_fusion, f32[256,128]{1,0:T(8,128)S(1)} %get-tuple-element.8, f32[256,128]{1,0:T(8,128)S(1)} %get-tuple-element.9), kind=kOutput, calls=%fused_computation.41 | convolution fusion | flops 202178560 | bytes 1572864 | tf_op jit(solution)/shard_map/kn,ckm->cnm/dot_general | solution.py:18
  66.2 1.4 %fusion.2 = f32[4,128,128]{1,2,0:T(8,128)S(1)} fusion(f32[4,128,128]{2,1,0:T(8,128)S(1)} %fusion.26, f32[4,256,128]{2,1,0:T(8,128)S(1)} %convolution_add_fusion, f32[4,256,128]{2,1,0:T(8,128)S(1)} %convolution_subtract_fusion, f32[256,128]{1,0:T(8,128)S(1)} %get-tuple-element.8, f32[256,128]{1,0:T(8,128)S(1)} %get-tuple-element.9), kind=kOutput, calls=%fused_computation.17 | convolution fusion | flops 202309632 | bytes 1835008 | tf_op jit(solution)/shard_map/kn,ckm->cnm/dot_general | solution.py:18
  68.5 3.9 %all-to-all-done.1 = bf16[4,16,1024]{2,0,1:T(4,128)(2,1)S(1)} async-done(((bf16[4,16,1024]{2,0,1:T(4,128)(2,1)}), bf16[4,16,1024]{2,0,1:T(4,128)(2,1)S(1)}, u32[]{:S(2)}, u32[]{:S(2)}) %all-to-all-start.1) | async-done | bytes 131104 | tf_op jit(solution)/shard_map/all_to_all | solution.py:80
  (29 shorter events, 14.7 us)
Async XLA Ops:
  2.2 17.2 %copy-start = (f32[1,4,16384]{2,1,0:T(4,128)S(1)}, f32[1,4,16384]{2,1,0:T(4,128)}, u32[]{:S(2)}) copy-start(f32[1,4,16384]{2,1,0:T(4,128)} %param.5) | copy-start | bytes 786436
  2.2 24.4 %all-to-all-start = ((bf16[16,4,1024]{2,1,0:T(4,128)(2,1)}), bf16[16,4,1024]{2,1,0:T(4,128)(2,1)S(1)}, u32[]{:S(2)}, u32[]{:S(2)}) async-start(bf16[16,4,1024]{2,1,0:T(4,128)(2,1)} %all_to_all.36), calls=%async_computation | async-start | bytes 262144 | tf_op jit(solution)/shard_map/all_to_all | solution.py:74
  22.4 0.9 %copy-start.1 = (bf16[64,1024]{1,0:T(8,128)(2,1)S(1)}, bf16[64,1024]{1,0:T(8,128)(2,1)}, u32[]{:S(2)}) copy-start(bf16[64,1024]{1,0:T(8,128)(2,1)} %param.3) | copy-start | bytes 393220
  26.6 14.2 %all-to-all-start.2 = ((bf16[16,4,1024]{2,1,0:T(4,128)(2,1)}), bf16[16,4,1024]{2,1,0:T(4,128)(2,1)S(1)}, u32[]{:S(2)}, u32[]{:S(2)}) async-start(bf16[16,4,1024]{2,1,0:T(4,128)(2,1)} %all_to_all.42), calls=%async_computation.2 | async-start | bytes 262144 | tf_op jit(solution)/shard_map/all_to_all | solution.py:73
  60.0 12.4 %all-to-all-start.1 = ((bf16[4,16,1024]{2,0,1:T(4,128)(2,1)}), bf16[4,16,1024]{2,0,1:T(4,128)(2,1)S(1)}, u32[]{:S(2)}, u32[]{:S(2)}) async-start(bf16[4,16,1024]{2,0,1:T(4,128)(2,1)} %copy.32), calls=%async_computation.1 | async-start | bytes 262144 | tf_op jit(solution)/shard_map/all_to_all | solution.py:80
where the time goes:
time: 73.5 us; the launch traced here: 73.1 us
  starting transfers between devices  28 us (38%)
  matrix products  27.7 us (38%)
  waiting for transfers between devices  10.7 us (15%)
  local copies, waits for them, and re-layouts  5.2 us (7%)
  between operations  0.92 us (1%)
    dot_general x30, matrix products, product(): jnp.einsum(pattern, left_operand, right_operand, precision=lax.Precision....  27.7 us
    all_to_all x1, starting transfers between devices, shards(): lax.all_to_all(grad_output, 'ctx', split_axis=0, concat_axis=1, tiled=True)  16.6 us
    all_to_all x1, starting transfers between devices, shards(): lax.all_to_all(layer_input, 'ctx', split_axis=0, concat_axis=1, tiled=True)  6.64 us
    all_to_all x1, waiting for transfers between devices, shards(): lax.all_to_all(layer_input, 'ctx', split_axis=0, concat_axis=1, tiled=True)  5.84 us
    all_to_all x1, starting transfers between devices, shards(): lax.all_to_all(local_back, 'ctx', split_axis=1, concat_axis=0, tiled=True)  4.76 us
    all_to_all x1, waiting for transfers between devices, shards(): lax.all_to_all(local_back, 'ctx', split_axis=1, concat_axis=0, tiled=True)  3.92 us
    all_to_all x2, local copies, waits for them, and re-layouts, shards(): lax.all_to_all(grad_output, 'ctx', split_axis=0, concat_axis=1, tiled=True)  1.66 us
  transfers between devices with their start and end apart: 3, of which 3 were waited for; matrix products, arithmetic and copies ran while one was open for 16% of the time, Pallas kernels for 0%

commit v1 on v0

v1 whole, which is shorter than its diff:
```python
import math

import jax
import jax.numpy as jnp
import numpy as np
from jax import lax
from jax.experimental import pallas as pl
from jax.experimental.pallas import tpu as pltpu
from jax.sharding import PartitionSpec as P

import ml_dtypes

BF = jnp.bfloat16
F32 = jnp.float32
SIDE = 128
PEERS = 16
PENCIL = 4
MESH = pl.DeviceIdType.MESH


def split_table(values):
    high = values.astype(ml_dtypes.bfloat16)
    low = (values - high.astype(np.float64)).astype(ml_dtypes.bfloat16)
    return high, low


def make_tables():
    total = SIDE * SIDE
    index = np.arange(SIDE, dtype=np.int64)
    first = ((4 * index[:, None] + 1) * index[None, :]) % (4 * SIDE) * (2.0 * np.pi / (4 * SIDE))
    first_high, first_low = split_table(np.concatenate([np.cos(first), -np.sin(first)], axis=0))
    forward_first = np.concatenate([first_high, first_low, first_high], axis=1)
    turn = ((4 * index[:, None] + 1) * index[None, :]) % (4 * total) * (2.0 * np.pi / (4 * total))
    turns = np.stack([np.cos(turn), np.sin(turn)]).astype(np.float32)
    second = (index[:, None] * index[None, :]) % SIDE * (2.0 * np.pi / SIDE)
    cos_two, sin_two = np.cos(second), np.sin(second)
    high, low = split_table(np.block([[cos_two, -sin_two], [sin_two, cos_two]]))
    forward_second = np.concatenate([high, high, low], axis=0)
    high, low = split_table(np.block([[cos_two, sin_two], [-sin_two, cos_two]]))
    inverse_second = np.concatenate([high, high, low], axis=0)
    high, low = split_table(np.concatenate([np.cos(first).T, -np.sin(first).T], axis=1) / total)
    inverse_first = np.concatenate([high, high, low], axis=1)
    return forward_first, forward_second, inverse_second, inverse_first, turns


def halves(value):
    high = value.astype(BF)
    return high, (value - high.astype(F32)).astype(BF)


def second_stage(first, turns_v, second_v):
    real, imag = first[:SIDE], first[SIDE:]
    cos_turn, sin_turn = turns_v[0], turns_v[1]
    real_high, real_low = halves(real * cos_turn + imag * sin_turn)
    imag_high, imag_low = halves(imag * cos_turn - real * sin_turn)
    stacked = jnp.concatenate([real_high, imag_high, real_low, imag_low, real_high, imag_high], axis=1)
    return jnp.dot(stacked, second_v[...], preferred_element_type=F32)


def inverse(real, imag, turns_v, inverse_second_v, inverse_first_v):
    real_high, real_low = halves(real)
    imag_high, imag_low = halves(imag)
    stacked = jnp.concatenate([real_high, imag_high, real_low, imag_low, real_high, imag_high], axis=1)
    mixed = jnp.dot(stacked, inverse_second_v[...], preferred_element_type=F32)
    real, imag = mixed[:, :SIDE], mixed[:, SIDE:]
    cos_turn, sin_turn = turns_v[0], turns_v[1]
    real_high, real_low = halves(real * cos_turn - imag * sin_turn)
    imag_high, imag_low = halves(imag * cos_turn + real * sin_turn)
    stacked = jnp.concatenate([real_high, imag_high, real_low, imag_low, real_high, imag_high], axis=0)
    return jnp.dot(inverse_first_v[...], stacked, preferred_element_type=F32)


def kernel(
    grad_hbm,
    input_hbm,
    taps_hbm,
    first_hbm,
    second_hbm,
    inverse_second_hbm,
    inverse_first_hbm,
    turns_hbm,
    grad_input_v,
    grad_taps_v,
    grad_v,
    input_v,
    taps_v,
    first_v,
    second_v,
    inverse_second_v,
    inverse_first_v,
    turns_v,
    turned_v,
    send_grad,
    send_input,
    send_back,
    got_grad,
    got_input,
    got_back,
    taps_spec,
    grad_spec,
    local_sem,
    send_sem,
    recv_sem,
):
    me = lax.axis_index("ctx")

    def load(source, target, slot):
        copy = pltpu.make_async_copy(source, target, local_sem.at[slot])
        copy.start()
        return copy

    grad_load = load(grad_hbm, grad_v, 0)
    input_load = load(input_hbm, input_v, 1)
    later_loads = [
        load(source, target, slot)
        for slot, (source, target) in enumerate(
            (
                (taps_hbm, taps_v),
                (first_hbm, first_v),
                (turns_hbm, turns_v),
                (second_hbm, second_v),
                (inverse_second_hbm, inverse_second_v),
                (inverse_first_hbm, inverse_first_v),
            ),
            2,
        )
    ]

    barrier = pltpu.get_barrier_semaphore()

    @pl.loop(1, PEERS)
    def _(step):
        pl.semaphore_signal(
            barrier, inc=1, device_id={"ctx": lax.rem(me + step, PEERS)}, device_id_type=MESH
        )

    def turn_rows(source, target):
        for group in range(8):
            turned_v[group] = source[group].astype(F32).reshape(64, SIDE)
            for row in range(8):
                picked = turned_v[group, pl.ds(row, 8, stride=8), :]
                target[2 * group + row // 4, row % 4] = picked.astype(BF)

    def exchange(source, target, slot):
        @pl.loop(1, PEERS)
        def _(step):
            peer = lax.rem(me + step, PEERS)
            pltpu.make_async_remote_copy(
                src_ref=source.at[peer],
                dst_ref=target.at[me],
                send_sem=send_sem.at[slot],
                recv_sem=recv_sem.at[slot],
                device_id={"ctx": peer},
                device_id_type=MESH,
            ).start()

        target[me] = source[me]

    def all_of(source, target, slot):
        return pltpu.make_async_remote_copy(
            src_ref=source.at[pl.ds(0, PEERS - 1)],
            dst_ref=target.at[pl.ds(0, PEERS - 1)],
            send_sem=send_sem.at[slot],
            recv_sem=recv_sem.at[slot],
            device_id={"ctx": lax.rem(me + 1, PEERS)},
            device_id_type=MESH,
        )

    grad_load.wait()
    turn_rows(grad_v, send_grad)
    pl.semaphore_wait(barrier, PEERS - 1)
    exchange(send_grad, got_grad, 0)
    input_load.wait()
    turn_rows(input_v, send_input)
    exchange(send_input, got_input, 1)

    for copy in later_loads:
        copy.wait()

    for channel in range(PENCIL):
        high, low = halves(taps_v[pl.ds(channel, SIDE, stride=PENCIL), :])
        first = jnp.dot(
            first_v[...], jnp.concatenate([high, high, low], axis=0), preferred_element_type=F32
        )
        taps_spec[channel] = second_stage(first, turns_v, second_v)

    def forward(source, channel):
        rows = source[:, channel].reshape(SIDE, SIDE)
        first = jnp.dot(
            first_v[:, : 2 * SIDE], jnp.concatenate([rows, rows], axis=0), preferred_element_type=F32
        )
        return second_stage(first, turns_v, second_v)

    all_of(send_grad, got_grad, 0).wait_recv()
    for channel in range(PENCIL):
        spectrum = forward(got_grad, channel)
        grad_spec[channel] = spectrum
        grad_real, grad_imag = spectrum[:, :SIDE], spectrum[:, SIDE:]
        taps_real, taps_imag = taps_spec[channel, :, :SIDE], taps_spec[channel, :, SIDE:]
        back = inverse(
            taps_real * grad_real + taps_imag * grad_imag,
            taps_real * grad_imag - taps_imag * grad_real,
            turns_v,
            inverse_second_v,
            inverse_first_v,
        )
        send_back[:, channel] = back.astype(BF).reshape(PEERS, 8, SIDE)
    exchange(send_back, got_back, 2)

    all_of(send_input, got_input, 1).wait_recv()
    for channel in range(PENCIL):
        spectrum = forward(got_input, channel)
        input_real, input_imag = spectrum[:, :SIDE], spectrum[:, SIDE:]
        grad_real, grad_imag = grad_spec[channel, :, :SIDE], grad_spec[channel, :, SIDE:]
        lags = inverse(
            grad_real * input_real + grad_imag * input_imag,
            grad_imag * input_real - grad_real * input_imag,
            turns_v,
            inverse_second_v,
            inverse_first_v,
        )
        grad_taps_v[pl.ds(channel, SIDE, stride=PENCIL), :] = lags * (1.0 / SIDE)

    all_of(send_back, got_back, 2).wait_recv()
    for group in range(8):
        for row in range(8):
            turned_v[group, pl.ds(8 * row, 8), :] = got_back[2 * group + row // 4, row % 4].astype(F32)
        for block in range(8):
            grad_input_v[group, block] = turned_v[group, pl.ds(block, 8, stride=8), :].astype(BF)
    for slot, (source, target) in enumerate(
        ((send_grad, got_grad), (send_input, got_input), (send_back, got_back))
    ):
        all_of(source, target, slot).wait_send()


def shards(layer_input, grad_output, filter_taps):
    rows, width = layer_input.shape
    blocks = width // SIDE
    tiles = (rows // 8, 8, blocks, SIDE)
    tables = make_tables()
    taps = filter_taps.reshape(PENCIL, SIDE, SIDE).transpose(1, 0, 2).reshape(PENCIL * SIDE, SIDE)
    tile_shape = (rows // 8, blocks, 8, SIDE)
    block_shape = (PEERS, PENCIL, blocks, SIDE)
    operands = (
        grad_output.reshape(tiles).transpose(0, 2, 1, 3),
        layer_input.reshape(tiles).transpose(0, 2, 1, 3),
        taps,
        *[jnp.asarray(table) for table in tables],
    )
    grad_input, grad_taps = pl.pallas_call(
        kernel,
        name="conv_backward",
        out_shape=(
            pltpu.VMEM(tile_shape, BF),
            pltpu.VMEM((PENCIL * SIDE, SIDE), F32),
        ),
        in_specs=[pl.BlockSpec(memory_space=pltpu.HBM)] * 8,
        out_specs=[pl.BlockSpec(memory_space=pltpu.VMEM)] * 2,
        scratch_shapes=[
            pltpu.VMEM(tile_shape, BF),
            pltpu.VMEM(tile_shape, BF),
            pltpu.VMEM((PENCIL * SIDE, SIDE), F32),
            *[pltpu.VMEM(table.shape, F32 if table.dtype == np.float32 else BF) for table in tables],
            pltpu.VMEM((8, 64, SIDE), F32),
            *[pltpu.VMEM(block_shape, BF)] * 6,
            pltpu.VMEM((PENCIL, SIDE, 2 * SIDE), F32),
            pltpu.VMEM((PENCIL, SIDE, 2 * SIDE), F32),
            pltpu.SemaphoreType.DMA((8,)),
            pltpu.SemaphoreType.DMA((3,)),
            pltpu.SemaphoreType.DMA((3,)),
        ],
        compiler_params=pltpu.CompilerParams(
            collective_id=0, has_side_effects=True, vmem_limit_bytes=48 * 1024 * 1024
        ),
    )(*[pltpu.with_memory_space_constraint(operand, pltpu.HBM) for operand in operands])
    grad_input = grad_input.transpose(0, 2, 1, 3).reshape(rows, width)
    grad_taps = grad_taps.reshape(SIDE, PENCIL, SIDE).transpose(1, 0, 2)
    return grad_input, grad_taps.reshape(1, PENCIL, SIDE * SIDE)


def solution(mesh):
    in_specs = (P(("dp", "chan"), "ctx"), P(("dp", "chan"), "ctx"), P(("dp", "chan"), "ctx", None))
    out_specs = (P(("dp", "chan"), "ctx"), P(("dp", "chan"), "ctx", None))
    return jax.shard_map(shards, mesh=mesh, in_specs=in_specs, out_specs=out_specs, check_vma=False)
```

time: 73.5 us -> 30.7 us (0.42)
  Pallas kernels: 0 us -> 28.5 us
  starting transfers between devices: 28 us -> 0 us
  matrix products: 27.7 us -> 0 us
  waiting for transfers between devices: 10.7 us -> 0 us
  local copies, waits for them, and re-layouts: 5.2 us -> 1.36 us
    pallas_call x0 -> x1, Pallas kernels: none -> 28.5 us  [shards(): pl.pallas_call(kernel, name='conv_backward', out_shape=(pltpu.VMEM(tile_s...]
    all_to_all x3 -> x0, starting transfers between devices: 28 us -> none  [the longest x1 16.6 us: shards(): lax.all_to_all(grad_output, 'ctx', split_axis=0, concat_axis=1, tiled=True)]
    dot_general x30 -> x0, matrix products: 27.7 us -> none  [product(): jnp.einsum(pattern, left_operand, right_operand, precision=lax.Precision....]
    all_to_all x3 -> x0, waiting for transfers between devices: 10.7 us -> none  [the longest x1 5.84 us: shards(): lax.all_to_all(layer_input, 'ctx', split_axis=0, concat_axis=1, tiled=True)]
    all_to_all x5 -> x0, local copies, waits for them, and re-layouts: 3.1 us -> none  [the longest x2 1.66 us: shards(): lax.all_to_all(grad_output, 'ctx', split_axis=0, concat_axis=1, tiled=True)]
    unnamed x4 -> x2, local copies, waits for them, and re-layouts: 0.07 us -> 1.36 us
    convert_element_type x3 -> x0, local copies, waits for them, and re-layouts: 0.95 us -> none  [shards(): inverse(back_real, back_imag, tables).reshape(pencil, length)]
    reshape x3 -> x0, local copies, waits for them, and re-layouts: 0.94 us -> none  [the longest x1 0.82 us: shards(): return (grad_input, local_taps.reshape(1, pencil, length))]
  transfers between devices with their start and end apart: 3 -> 0, of which waited for: 3 -> 0; matrix products, arithmetic and copies ran while one was open for 16% -> 0% of each run, Pallas kernels for 0% -> 0%
where the time goes in v1:
time: 30.7 us; the launch traced here: 30.5 us
  Pallas kernels  28.5 us (93%)
  local copies, waits for them, and re-layouts  1.36 us (4%)
  between operations  0.64 us (2%)
    pallas_call x1, Pallas kernels, shards(): pl.pallas_call(kernel, name='conv_backward', out_shape=(pltpu.VMEM(tile_s...  28.5 us
    unnamed x2, local copies, waits for them, and re-layouts  1.36 us

profile of v1, /device:TPU:2, one launch (start us, length us, event | category | flops | bytes accessed | tf_op | source)
XLA Modules:
  0.0 30.5 jit_solution(2718045606354864452)
XLA Ops:
  0.6 28.5 %conv_backward.1 = (bf16[8,8,8,128]{3,2,1,0:T(8,128)(2,1)S(1)}, f32[512,128]{1,0:T(8,128)S(1)}) custom-call(bf16[8,8,8,128]{3,2,1,0:T(8,128)(2,1)} %bitcast.22, bf16[8,8,8,128]{3,2,1,0:T(8,128)(2,1)} %bitcast.23, f32[512,128]{1,0:T(8,128)} %bitcast.21, bf16[256,384]{1,0:T(8,128)(2,1)} %constant.10.clone.first_hbm, ...), custom_call_target="tpu_custom_call" | custom-call | tf_op jit(solution)/shard_map/conv_backward/pallas_call | solution.py:250
  29.1 0.7 %copy.14 = bf16[64,1024]{1,0:T(8,128)(2,1)} copy(bf16[64,1024]{1,0:T(8,128)(2,1)S(1)} %bitcast.20) | data formatting | bytes 262144
  29.8 0.7 %copy.15 = f32[1,4,16384]{2,1,0:T(4,128)} copy(f32[1,4,16384]{2,1,0:T(4,128)S(1)} %bitcast.19) | data formatting | bytes 524288

commit v2 on v1

--- a/solution.py
+++ b/solution.py
@@ -15,7 +15,12 @@
 SIDE = 128
 PEERS = 16
 PENCIL = 4
+BATCH = 4
 MESH = pl.DeviceIdType.MESH
+FAR_FIRST = (
+    (3, 2), (3, 1), (3, 3), (2, 2), (2, 1), (2, 3), (3, 0), (1, 2),
+    (2, 0), (1, 1), (1, 3), (0, 2), (1, 0), (0, 1), (0, 3),
+)
 
 
 def split_table(values):
@@ -48,26 +53,42 @@
     return high, (value - high.astype(F32)).astype(BF)
 
 
+def stacked_rows(pairs, turned):
+    blocks = []
+    for real, imag in pairs:
+        real_high, real_low = halves(real)
+        imag_high, imag_low = halves(imag)
+        parts = [real_high, imag_high, real_low, imag_low, real_high, imag_high]
+        blocks.append(jnp.concatenate(parts, axis=0 if turned else 1))
+    return jnp.concatenate(blocks, axis=1 if turned else 0)
+
+
+def channel_parts(spectra):
+    count = spectra.shape[0] // SIDE
+    return [
+        (spectra[at * SIDE : (at + 1) * SIDE, :SIDE], spectra[at * SIDE : (at + 1) * SIDE, SIDE:])
+        for at in range(count)
+    ]
+
+
 def second_stage(first, turns_v, second_v):
-    real, imag = first[:SIDE], first[SIDE:]
     cos_turn, sin_turn = turns_v[0], turns_v[1]
-    real_high, real_low = halves(real * cos_turn + imag * sin_turn)
-    imag_high, imag_low = halves(imag * cos_turn - real * sin_turn)
-    stacked = jnp.concatenate([real_high, imag_high, real_low, imag_low, real_high, imag_high], axis=1)
-    return jnp.dot(stacked, second_v[...], preferred_element_type=F32)
-
-
-def inverse(real, imag, turns_v, inverse_second_v, inverse_first_v):
-    real_high, real_low = halves(real)
-    imag_high, imag_low = halves(imag)
-    stacked = jnp.concatenate([real_high, imag_high, real_low, imag_low, real_high, imag_high], axis=1)
-    mixed = jnp.dot(stacked, inverse_second_v[...], preferred_element_type=F32)
-    real, imag = mixed[:, :SIDE], mixed[:, SIDE:]
+    pairs = []
+    for at in range(first.shape[1] // SIDE):
+        real = first[:SIDE, at * SIDE : (at + 1) * SIDE]
+        imag = first[SIDE:, at * SIDE : (at + 1) * SIDE]
+        pairs.append((real * cos_turn + imag * sin_turn, imag * cos_turn - real * sin_turn))
+    return jnp.dot(stacked_rows(pairs, False), second_v[...], preferred_element_type=F32)
+
+
+def inverse(pairs, turns_v, inverse_second_v, inverse_first_v):
+    mixed = jnp.dot(stacked_rows(pairs, False), inverse_second_v[...], preferred_element_type=F32)
     cos_turn, sin_turn = turns_v[0], turns_v[1]
-    real_high, real_low = halves(real * cos_turn - imag * sin_turn)
-    imag_high, imag_low = halves(imag * cos_turn + real * sin_turn)
-    stacked = jnp.concatenate([real_high, imag_high, real_low, imag_low, real_high, imag_high], axis=0)
-    return jnp.dot(inverse_first_v[...], stacked, preferred_element_type=F32)
+    turned = [
+        (real * cos_turn - imag * sin_turn, imag * cos_turn + real * sin_turn)
+        for real, imag in channel_parts(mixed)
+    ]
+    return jnp.dot(inverse_first_v[...], stacked_rows(turned, True), preferred_element_type=F32)
 
 
 def kernel(
@@ -79,7 +100,7 @@
     inverse_second_hbm,
     inverse_first_hbm,
     turns_hbm,
-    grad_input_v,
+    got_back,
     grad_taps_v,
     grad_v,
     input_v,
@@ -95,7 +116,6 @@
     send_back,
     got_grad,
     got_input,
-    got_back,
     taps_spec,
     grad_spec,
     local_sem,
@@ -103,6 +123,9 @@
     recv_sem,
 ):
     me = lax.axis_index("ctx")
+    row, column = me // 4, me % 4
+    rows = (row, row + 1 - 2 * (row % 2), (row + 2) % 4, 3 - row)
+    peers = [rows[over] * 4 + (column + along) % 4 for over, along in FAR_FIRST]
 
     def load(source, target, slot):
         copy = pltpu.make_async_copy(source, target, local_sem.at[slot])
@@ -128,11 +151,8 @@
 
     barrier = pltpu.get_barrier_semaphore()
 
-    @pl.loop(1, PEERS)
-    def _(step):
-        pl.semaphore_signal(
-            barrier, inc=1, device_id={"ctx": lax.rem(me + step, PEERS)}, device_id_type=MESH
-        )
+    for peer in peers:
+        pl.semaphore_signal(barrier, inc=1, device_id={"ctx": peer}, device_id_type=MESH)
 
     def turn_rows(source, target):
         for group in range(8):
@@ -142,9 +162,7 @@
                 target[2 * group + row // 4, row % 4] = picked.astype(BF)
 
     def exchange(source, target, slot):
-        @pl.loop(1, PEERS)
-        def _(step):
-            peer = lax.rem(me + step, PEERS)
+        for peer in peers:
             pltpu.make_async_remote_copy(
                 src_ref=source.at[peer],
                 dst_ref=target.at[me],
@@ -177,60 +195,75 @@
     for copy in later_loads:
         copy.wait()
 
-    for channel in range(PENCIL):
-        high, low = halves(taps_v[pl.ds(channel, SIDE, stride=PENCIL), :])
+    for start in range(0, PENCIL, BATCH):
+        columns = []
+        for channel in range(start, start + BATCH):
+            high, low = halves(taps_v[pl.ds(channel, SIDE, stride=PENCIL), :])
+            columns.append(jnp.concatenate([high, high, low], axis=0))
         first = jnp.dot(
-            first_v[...], jnp.concatenate([high, high, low], axis=0), preferred_element_type=F32
-        )
-        taps_spec[channel] = second_stage(first, turns_v, second_v)
-
-    def forward(source, channel):
-        rows = source[:, channel].reshape(SIDE, SIDE)
+            first_v[...], jnp.concatenate(columns, axis=1), preferred_element_type=F32
+        )
+        taps_spec[start * SIDE : (start + BATCH) * SIDE, :] = second_stage(first, turns_v, second_v)
+
+    def forward(source, start):
+        rows = jnp.concatenate(
+            [source[:, channel].reshape(SIDE, SIDE) for channel in range(start, start + BATCH)], axis=1
+        )
         first = jnp.dot(
             first_v[:, : 2 * SIDE], jnp.concatenate([rows, rows], axis=0), preferred_element_type=F32
         )
         return second_stage(first, turns_v, second_v)
 
     all_of(send_grad, got_grad, 0).wait_recv()
-    for channel in range(PENCIL):
-        spectrum = forward(got_grad, channel)
-        grad_spec[channel] = spectrum
-        grad_real, grad_imag = spectrum[:, :SIDE], spectrum[:, SIDE:]
-        taps_real, taps_imag = taps_spec[channel, :, :SIDE], taps_spec[channel, :, SIDE:]
-        back = inverse(
-            taps_real * grad_real + taps_imag * grad_imag,
-            taps_real * grad_imag - taps_imag * grad_real,
-            turns_v,
-            inverse_second_v,
-            inverse_first_v,
-        )
-        send_back[:, channel] = back.astype(BF).reshape(PEERS, 8, SIDE)
+    for start in range(0, PENCIL, BATCH):
+        spectra = forward(got_grad, start)
+        grad_spec[start * SIDE : (start + BATCH) * SIDE, :] = spectra
+        products = [
+            (taps_real * real + taps_imag * imag, taps_real * imag - taps_imag * real)
+            for (real, imag), (taps_real, taps_imag) in zip(
+                channel_parts(spectra),
+                channel_parts(taps_spec[start * SIDE : (start + BATCH) * SIDE, :]),
+            )
+        ]
+        back = inverse(products, turns_v, inverse_second_v, inverse_first_v).astype(BF)
+        for at in range(BATCH):
+            block = back[:, at * SIDE : (at + 1) * SIDE]
+            send_back[:, start + at] = block.reshape(PEERS, 8, SIDE)
     exchange(send_back, got_back, 2)
 
     all_of(send_input, got_input, 1).wait_recv()
-    for channel in range(PENCIL):
-        spectrum = forward(got_input, channel)
-        input_real, input_imag = spectrum[:, :SIDE], spectrum[:, SIDE:]
-        grad_real, grad_imag = grad_spec[channel, :, :SIDE], grad_spec[channel, :, SIDE:]
-        lags = inverse(
-            grad_real * input_real + grad_imag * input_imag,
-            grad_imag * input_real - grad_real * input_imag,
-            turns_v,
-            inverse_second_v,
-            inverse_first_v,
-        )
-        grad_taps_v[pl.ds(channel, SIDE, stride=PENCIL), :] = lags * (1.0 / SIDE)
+    for start in range(0, PENCIL, BATCH):
+        spectra = forward(got_input, start)
+        products = [
+            (grad_real * real + grad_imag * imag, grad_imag * real - grad_real * imag)
+            for (real, imag), (grad_real, grad_imag) in zip(
+                channel_parts(spectra),
+                channel_parts(grad_spec[start * SIDE : (start + BATCH) * SIDE, :]),
+            )
+        ]
+        lags = inverse(products, turns_v, inverse_second_v, inverse_first_v) * (1.0 / SIDE)
+        for at in range(BATCH):
+            grad_taps_v[pl.ds(start + at, SIDE, stride=PENCIL), :] = lags[:, at * SIDE : (at + 1) * SIDE]
 
     all_of(send_back, got_back, 2).wait_recv()
+    for slot, (source, target) in enumerate(
+        ((send_grad, got_grad), (send_input, got_input), (send_back, got_back))
+    ):
+        all_of(source, target, slot).wait_send()
+
+
+def finish(got_back, grad_taps_v, grad_input_hbm, grad_taps_hbm, turned_v, grad_input_v, sem):
+    taps_store = pltpu.make_async_copy(grad_taps_v, grad_taps_hbm, sem.at[0])
+    taps_store.start()
     for group in range(8):
         for row in range(8):
             turned_v[group, pl.ds(8 * row, 8), :] = got_back[2 * group + row // 4, row % 4].astype(F32)
         for block in range(8):
             grad_input_v[group, block] = turned_v[group, pl.ds(block, 8, stride=8), :].astype(BF)
-    for slot, (source, target) in enumerate(
-        ((send_grad, got_grad), (send_input, got_input), (send_back, got_back))
-    ):
-        all_of(source, target, slot).wait_send()
+    back_store = pltpu.make_async_copy(grad_input_v, grad_input_hbm, sem.at[1])
+    back_store.start()
+    taps_store.wait()
+    back_store.wait()
 
 
 def shards(layer_input, grad_output, filter_taps):
@@ -247,11 +280,11 @@
         taps,
         *[jnp.asarray(table) for table in tables],
     )
-    grad_input, grad_taps = pl.pallas_call(
+    back_blocks, lags = pl.pallas_call(
         kernel,
         name="conv_backward",
         out_shape=(
-            pltpu.VMEM(tile_shape, BF),
+            pltpu.VMEM(block_shape, BF),
             pltpu.VMEM((PENCIL * SIDE, SIDE), F32),
         ),
         in_specs=[pl.BlockSpec(memory_space=pltpu.HBM)] * 8,
@@ -262,9 +295,9 @@
             pltpu.VMEM((PENCIL * SIDE, SIDE), F32),
             *[pltpu.VMEM(table.shape, F32 if table.dtype == np.float32 else BF) for table in tables],
             pltpu.VMEM((8, 64, SIDE), F32),
-            *[pltpu.VMEM(block_shape, BF)] * 6,
-            pltpu.VMEM((PENCIL, SIDE, 2 * SIDE), F32),
-            pltpu.VMEM((PENCIL, SIDE, 2 * SIDE), F32),
+            *[pltpu.VMEM(block_shape, BF)] * 5,
+            pltpu.VMEM((PENCIL * SIDE, 2 * SIDE), F32),
+            pltpu.VMEM((PENCIL * SIDE, 2 * SIDE), F32),
             pltpu.SemaphoreType.DMA((8,)),
             pltpu.SemaphoreType.DMA((3,)),
             pltpu.SemaphoreType.DMA((3,)),
@@ -273,6 +306,21 @@
             collective_id=0, has_side_effects=True, vmem_limit_bytes=48 * 1024 * 1024
         ),
     )(*[pltpu.with_memory_space_constraint(operand, pltpu.HBM) for operand in operands])
+    grad_input, grad_taps = pl.pallas_call(
+        finish,
+        name="conv_backward_finish",
+        out_shape=(
+            jax.ShapeDtypeStruct(tile_shape, BF),
+            jax.ShapeDtypeStruct((PENCIL * SIDE, SIDE), F32),
+        ),
+        in_specs=[pl.BlockSpec(memory_space=pltpu.VMEM)] * 2,
+        out_specs=[pl.BlockSpec(memory_space=pltpu.HBM)] * 2,
+        scratch_shapes=[
+            pltpu.VMEM((8, 64, SIDE), F32),
+            pltpu.VMEM(tile_shape, BF),
+            pltpu.SemaphoreType.DMA((2,)),
+        ],
+    )(*[pltpu.with_memory_space_constraint(operand, pltpu.VMEM) for operand in (back_blocks, lags)])
     grad_input = grad_input.transpose(0, 2, 1, 3).reshape(rows, width)
     grad_taps = grad_taps.reshape(SIDE, PENCIL, SIDE).transpose(1, 0, 2)
     return grad_input, grad_taps.reshape(1, PENCIL, SIDE * SIDE)

time: 30.7 us -> 28.3 us (0.922)
  the two profiles are of different devices: /device:TPU:2 before, /device:TPU:8 now
where the time goes in v2:
time: 28.3 us; the launch traced here: 28.2 us
  Pallas kernels  27.5 us (97%)
  between operations  0.64 us (2%)
    pallas_call x1, Pallas kernels, shards(): pl.pallas_call(kernel, name='conv_backward', out_shape=(pltpu.VMEM(block_...  26.8 us
    pallas_call x1, Pallas kernels, shards(): pl.pallas_call(finish, name='conv_backward_finish', out_shape=(jax.ShapeD...  0.76 us

profile of v2, /device:TPU:8, one launch (start us, length us, event | category | flops | bytes accessed | tf_op | source)
XLA Modules:
  0.0 28.2 jit_solution(17039194279050117200)
XLA Ops:
  0.6 26.8 %conv_backward.1 = (bf16[16,4,8,128]{3,2,1,0:T(8,128)(2,1)S(1)}, f32[512,128]{1,0:T(8,128)S(1)}) custom-call(bf16[8,8,8,128]{3,2,1,0:T(8,128)(2,1)} %bitcast.20, bf16[8,8,8,128]{3,2,1,0:T(8,128)(2,1)} %bitcast.21, f32[512,128]{1,0:T(8,128)} %bitcast.19, bf16[256,384]{1,0:T(8,128)(2,1)} %constant.10.clone.first_hbm, ...), custom_call_target="tpu_custom_call" | custom-call | tf_op jit(solution)/shard_map/conv_backward/pallas_call | solution.py:283
  27.4 0.8 %conv_backward_finish.1 = (bf16[8,8,8,128]{3,2,1,0:T(8,128)(2,1)}, f32[512,128]{1,0:T(8,128)}) custom-call(bf16[16,4,8,128]{3,2,1,0:T(8,128)(2,1)S(1)} %get-tuple-element.6.got_back, f32[512,128]{1,0:T(8,128)S(1)} %get-tuple-element.7.grad_taps_v), custom_call_target="tpu_custom_call" | custom-call | tf_op jit(solution)/shard_map/conv_backward_finish/pallas_call | solution.py:309

commit v3 on v2

--- a/solution.py
+++ b/solution.py
@@ -14,8 +14,8 @@
 F32 = jnp.float32
 SIDE = 128
 PEERS = 16
+BLOCKS = 8
 PENCIL = 4
-BATCH = 4
 MESH = pl.DeviceIdType.MESH
 FAR_FIRST = (
     (3, 2), (3, 1), (3, 3), (2, 2), (2, 1), (2, 3), (3, 0), (1, 2),
@@ -45,7 +45,26 @@
     inverse_second = np.concatenate([high, high, low], axis=0)
     high, low = split_table(np.concatenate([np.cos(first).T, -np.sin(first).T], axis=1) / total)
     inverse_first = np.concatenate([high, high, low], axis=1)
-    return forward_first, forward_second, inverse_second, inverse_first, turns
+    short, each = index[:BLOCKS], np.eye(SIDE // BLOCKS)
+    first = ((4 * short[:, None] + 1) * short[None, :]) % (4 * BLOCKS) * (2.0 * np.pi / (4 * BLOCKS))
+    real, imag = np.kron(each, np.cos(first)), np.kron(each, -np.sin(first))
+    high, low = split_table(np.concatenate([real, imag], axis=0))
+    local_first = np.concatenate([high, low, high], axis=1)
+    high, low = split_table(np.concatenate([real.T, imag.T], axis=1) / (BLOCKS * SIDE))
+    local_inverse_first = np.concatenate([high, high, low], axis=1)
+    turn = (4 * short[:, None] + 1) * index[None, :] * (2.0 * np.pi / (4 * BLOCKS * SIDE))
+    turn = np.tile(turn, (SIDE // BLOCKS, 1))
+    local_turns = np.stack([np.cos(turn), np.sin(turn)]).astype(np.float32)
+    return (
+        forward_first,
+        turns,
+        forward_second,
+        inverse_second,
+        inverse_first,
+        local_first,
+        local_turns,
+        local_inverse_first,
+    )
 
 
 def halves(value):
@@ -91,38 +110,82 @@
     return jnp.dot(inverse_first_v[...], stacked_rows(turned, True), preferred_element_type=F32)
 
 
+def forward_wide(blocks, first_v, turns_v, second_v):
+    columns = []
+    for block in blocks:
+        high, low = halves(block)
+        columns.append(jnp.concatenate([high, high, low], axis=0))
+    first = jnp.dot(first_v[...], jnp.concatenate(columns, axis=1), preferred_element_type=F32)
+    return second_stage(first, turns_v, second_v)
+
+
+def forward(blocks, first_v, turns_v, second_v):
+    rows = jnp.concatenate(blocks, axis=1)
+    first = jnp.dot(
+        first_v[:, : 2 * SIDE], jnp.concatenate([rows, rows], axis=0), preferred_element_type=F32
+    )
+    return second_stage(first, turns_v, second_v)
+
+
+def correlation(taken, turned):
+    return [
+        (turned_real * real + turned_imag * imag, turned_real * imag - turned_imag * real)
+        for (real, imag), (turned_real, turned_imag) in zip(channel_parts(taken), channel_parts(turned))
+    ]
+
+
 def kernel(
     grad_hbm,
     input_hbm,
     taps_hbm,
     first_hbm,
+    turns_hbm,
     second_hbm,
     inverse_second_hbm,
     inverse_first_hbm,
-    turns_hbm,
+    local_first_hbm,
+    local_turns_hbm,
+    local_inverse_first_hbm,
     got_back,
     grad_taps_v,
     grad_v,
     input_v,
     taps_v,
     first_v,
+    turns_v,
     second_v,
     inverse_second_v,
     inverse_first_v,
-    turns_v,
+    local_first_v,
+    local_turns_v,
+    local_inverse_first_v,
     turned_v,
     send_grad,
     send_input,
     send_back,
     got_grad,
     got_input,
+    last_grad,
+    last_input,
+    pass_grad,
+    pass_input,
+    send_taps,
+    send_part,
+    got_taps,
+    got_part,
     taps_spec,
     grad_spec,
     local_sem,
     send_sem,
     recv_sem,
+    entered_sem,
 ):
-    me = lax.axis_index("ctx")
+    part, me, half = lax.axis_index("dp"), lax.axis_index("ctx"), lax.axis_index("chan")
+    in_group = (part == 0) & (half == 0)
+    is_last = in_group & (me == 0)
+    is_ahead = in_group & (me > 0)
+    is_pass = (part == 1) & (half == 0) & (me == 0)
+    last_id, pass_id = {"dp": 0, "ctx": 0}, {"dp": 1, "ctx": 0}
     row, column = me // 4, me % 4
     rows = (row, row + 1 - 2 * (row % 2), (row + 2) % 4, 3 - row)
     peers = [rows[over] * 4 + (column + along) % 4 for over, along in FAR_FIRST]
@@ -134,122 +197,226 @@
 
     grad_load = load(grad_hbm, grad_v, 0)
     input_load = load(input_hbm, input_v, 1)
-    later_loads = [
+    taps_load = load(taps_hbm, taps_v, 2)
+    table_loads = [
         load(source, target, slot)
         for slot, (source, target) in enumerate(
             (
-                (taps_hbm, taps_v),
                 (first_hbm, first_v),
                 (turns_hbm, turns_v),
                 (second_hbm, second_v),
                 (inverse_second_hbm, inverse_second_v),
                 (inverse_first_hbm, inverse_first_v),
+                (local_first_hbm, local_first_v),
+                (local_turns_hbm, local_turns_v),
+                (local_inverse_first_hbm, local_inverse_first_v),
             ),
-            2,
+            3,
         )
     ]
 
     barrier = pltpu.get_barrier_semaphore()
 
-    for peer in peers:
-        pl.semaphore_signal(barrier, inc=1, device_id={"ctx": peer}, device_id_type=MESH)
+    @pl.when(jnp.logical_not(is_last))
+    def _():
+        for peer in peers:
+            pl.semaphore_signal(barrier, inc=1, device_id={"ctx": peer}, device_id_type=MESH)
+
+    @pl.when(is_pass)
+    def _():
+        for peer in range(PEERS):
+            pl.semaphore_signal(barrier, inc=1, device_id={"dp": 0, "ctx": peer}, device_id_type=MESH)
 
     def turn_rows(source, target):
         for group in range(8):
             turned_v[group] = source[group].astype(F32).reshape(64, SIDE)
-            for row in range(8):
-                picked = turned_v[group, pl.ds(row, 8, stride=8), :]
-                target[2 * group + row // 4, row % 4] = picked.astype(BF)
+            for at in range(8):
+                picked = turned_v[group, pl.ds(at, 8, stride=8), :]
+                target[2 * group + at // 4, at % 4] = picked.astype(BF)
+
+    def send(source, target, sent, received, device):
+        return pltpu.make_async_remote_copy(
+            src_ref=source,
+            dst_ref=target,
+            send_sem=send_sem.at[sent],
+            recv_sem=recv_sem.at[received],
+            device_id=device,
+            device_id_type=MESH,
+        )
 
     def exchange(source, target, slot):
         for peer in peers:
-            pltpu.make_async_remote_copy(
-                src_ref=source.at[peer],
-                dst_ref=target.at[me],
-                send_sem=send_sem.at[slot],
-                recv_sem=recv_sem.at[slot],
-                device_id={"ctx": peer},
-                device_id_type=MESH,
-            ).start()
+
+            @pl.when(jnp.logical_not(is_ahead & (peer == 0)))
+            def _():
+                send(source.at[peer], target.at[me], slot, slot, {"ctx": peer}).start()
 
         target[me] = source[me]
 
-    def all_of(source, target, slot):
-        return pltpu.make_async_remote_copy(
-            src_ref=source.at[pl.ds(0, PEERS - 1)],
-            dst_ref=target.at[pl.ds(0, PEERS - 1)],
-            send_sem=send_sem.at[slot],
-            recv_sem=recv_sem.at[slot],
-            device_id={"ctx": lax.rem(me + 1, PEERS)},
-            device_id_type=MESH,
+    def gather(source, target, slot, last, passed):
+        @pl.when(is_last)
+        def _():
+            for peer in peers:
+                send(source.at[peer], last, slot, slot + 3, {"ctx": peer}).start()
+
+            target[me] = source[me]
+
+        @pl.when(jnp.logical_not(is_last))
+        def _():
+            exchange(source, target, slot)
+
+        @pl.when(is_ahead)
+        def _():
+            send(source.at[0], passed.at[me], slot + 3, slot + 5, pass_id).start()
+
+    def some_of(source, target, count, sent, received):
+        return send(
+            source.at[pl.ds(0, count)],
+            target.at[pl.ds(0, count)],
+            sent,
+            received,
+            {"ctx": peers[0]},
         )
+
+    def all_received(source, target, slot):
+        @pl.when(is_ahead)
+        def _():
+            some_of(source, target, PEERS - 2, slot, slot).wait_recv()
+
+        @pl.when(jnp.logical_not(is_ahead))
+        def _():
+            some_of(source, target, PEERS - 1, slot, slot).wait_recv()
 
     grad_load.wait()
     turn_rows(grad_v, send_grad)
-    pl.semaphore_wait(barrier, PEERS - 1)
-    exchange(send_grad, got_grad, 0)
+
+    @pl.when(jnp.logical_not(is_last))
+    def _():
+        pl.semaphore_wait(barrier, PEERS - 1)
+
+    @pl.when(is_last)
+    def _():
+        pl.semaphore_wait(barrier, PEERS)
+        pl.semaphore_signal(entered_sem, inc=1, device_id=pass_id, device_id_type=MESH)
+
+    gather(send_grad, got_grad, 0, last_grad, pass_grad)
     input_load.wait()
     turn_rows(input_v, send_input)
-    exchange(send_input, got_input, 1)
-
-    for copy in later_loads:
+    gather(send_input, got_input, 1, last_input, pass_input)
+
+    taps_load.wait()
+    for channel in range(PENCIL):
+        send_taps[channel] = taps_v[pl.ds(channel, BLOCKS, stride=PENCIL), :]
+
+    for copy in table_loads:
         copy.wait()
 
-    for start in range(0, PENCIL, BATCH):
-        columns = []
-        for channel in range(start, start + BATCH):
-            high, low = halves(taps_v[pl.ds(channel, SIDE, stride=PENCIL), :])
-            columns.append(jnp.concatenate([high, high, low], axis=0))
-        first = jnp.dot(
-            first_v[...], jnp.concatenate(columns, axis=1), preferred_element_type=F32
+    taps_spec[...] = forward_wide(
+        [taps_v[pl.ds(channel, SIDE, stride=PENCIL), :] for channel in range(PENCIL)],
+        first_v,
+        turns_v,
+        second_v,
+    )
+
+    def channels(source):
+        return [source[:, channel].reshape(SIDE, SIDE) for channel in range(PENCIL)]
+
+    all_received(send_grad, got_grad, 0)
+
+    @pl.when(is_ahead)
+    def _():
+        got_grad[0] = jnp.zeros_like(got_grad[0])
+
+    grad_spec[...] = forward(channels(got_grad), first_v, turns_v, second_v)
+    back = inverse(
+        correlation(grad_spec[...], taps_spec[...]), turns_v, inverse_second_v, inverse_first_v
+    )
+    for channel in range(PENCIL):
+        block = back[:, channel * SIDE : (channel + 1) * SIDE]
+        send_part[channel] = block[:BLOCKS]
+        send_back[:, channel] = block.astype(BF).reshape(PEERS, BLOCKS, SIDE)
+    exchange(send_back, got_back, 2)
+
+    all_received(send_input, got_input, 1)
+
+    @pl.when(is_ahead)
+    def _():
+        send(send_grad.at[0], last_grad, 0, 3, last_id).wait_recv()
+        send(send_input.at[0], last_input, 1, 4, last_id).wait_recv()
+        send(send_taps, got_taps.at[me], 5, 7, last_id).start()
+        send(send_part, got_part.at[me], 6, 8, last_id).start()
+        got_grad[0] = last_grad[...]
+        got_input[0] = last_input[...]
+        grad_spec[...] = forward(channels(got_grad), first_v, turns_v, second_v)
+
+    input_spec = forward(channels(got_input), first_v, turns_v, second_v)
+    lags = inverse(
+        correlation(grad_spec[...], input_spec), turns_v, inverse_second_v, inverse_first_v
+    ) * (1.0 / SIDE)
+    for channel in range(PENCIL):
+        grad_taps_v[pl.ds(channel, SIDE, stride=PENCIL), :] = lags[:, channel * SIDE : (channel + 1) * SIDE]
+
+    def others(ref):
+        return ref.at[pl.ds(1, PEERS - 1)]
+
+    passes = (
+        (pass_grad, got_grad, 7, 5, 0),
+        (pass_input, got_input, 8, 6, 1),
+    )
+
+    @pl.when(is_pass)
+    def _():
+        for at, (passed, target, sent, arrived, received) in enumerate(passes):
+            send(others(passed), others(passed), sent, arrived, last_id).wait_recv()
+            if at == 0:
+                pl.semaphore_wait(entered_sem, 1)
+            send(others(passed), others(target), sent, received, last_id).start()
+
+    @pl.when(is_last)
+    def _():
+        some_of(got_taps, got_taps, PEERS - 1, 5, 7).wait_recv()
+        got_taps[0] = send_taps[...]
+
+        def local_blocks(ref):
+            return [ref[at : at + 4].reshape(SIDE, SIDE) for at in range(0, PEERS, 4)]
+
+        local_taps = forward_wide(local_blocks(got_taps), local_first_v, local_turns_v, second_v)
+        local_grad = forward(local_blocks(send_grad), local_first_v, local_turns_v, second_v)
+        local = inverse(
+            correlation(local_grad, local_taps), local_turns_v, inverse_second_v, local_inverse_first_v
         )
-        taps_spec[start * SIDE : (start + BATCH) * SIDE, :] = second_stage(first, turns_v, second_v)
-
-    def forward(source, start):
-        rows = jnp.concatenate(
-            [source[:, channel].reshape(SIDE, SIDE) for channel in range(start, start + BATCH)], axis=1
-        )
-        first = jnp.dot(
-            first_v[:, : 2 * SIDE], jnp.concatenate([rows, rows], axis=0), preferred_element_type=F32
-        )
-        return second_stage(first, turns_v, second_v)
-
-    all_of(send_grad, got_grad, 0).wait_recv()
-    for start in range(0, PENCIL, BATCH):
-        spectra = forward(got_grad, start)
-        grad_spec[start * SIDE : (start + BATCH) * SIDE, :] = spectra
-        products = [
-            (taps_real * real + taps_imag * imag, taps_real * imag - taps_imag * real)
-            for (real, imag), (taps_real, taps_imag) in zip(
-                channel_parts(spectra),
-                channel_parts(taps_spec[start * SIDE : (start + BATCH) * SIDE, :]),
-            )
-        ]
-        back = inverse(products, turns_v, inverse_second_v, inverse_first_v).astype(BF)
-        for at in range(BATCH):
-            block = back[:, at * SIDE : (at + 1) * SIDE]
-            send_back[:, start + at] = block.reshape(PEERS, 8, SIDE)
-    exchange(send_back, got_back, 2)
-
-    all_of(send_input, got_input, 1).wait_recv()
-    for start in range(0, PENCIL, BATCH):
-        spectra = forward(got_input, start)
-        products = [
-            (grad_real * real + grad_imag * imag, grad_imag * real - grad_real * imag)
-            for (real, imag), (grad_real, grad_imag) in zip(
-                channel_parts(spectra),
-                channel_parts(grad_spec[start * SIDE : (start + BATCH) * SIDE, :]),
-            )
-        ]
-        lags = inverse(products, turns_v, inverse_second_v, inverse_first_v) * (1.0 / SIDE)
-        for at in range(BATCH):
-            grad_taps_v[pl.ds(start + at, SIDE, stride=PENCIL), :] = lags[:, at * SIDE : (at + 1) * SIDE]
-
-    all_of(send_back, got_back, 2).wait_recv()
+        some_of(got_part, got_part, PEERS - 1, 6, 8).wait_recv()
+        for at in range(1, PEERS):
+            block = local[:, at // 4 * SIDE : (at // 4 + 1) * SIDE].reshape(4, PENCIL, BLOCKS, SIDE)
+            got_back[at] = (got_part[at] + block[at % 4]).astype(BF)
+
+    @pl.when(jnp.logical_not(is_last))
+    def _():
+        some_of(send_back, got_back, PEERS - 1, 2, 2).wait_recv()
+
     for slot, (source, target) in enumerate(
         ((send_grad, got_grad), (send_input, got_input), (send_back, got_back))
     ):
-        all_of(source, target, slot).wait_send()
+
+        @pl.when(is_ahead)
+        def _():
+            some_of(source, target, PEERS - 2, slot, slot).wait_send()
+
+        @pl.when(jnp.logical_not(is_ahead))
+        def _():
+            some_of(source, target, PEERS - 1, slot, slot).wait_send()
+
+    @pl.when(is_ahead)
+    def _():
+        send(send_grad.at[0], last_grad, 3, 5, pass_id).wait_send()
+        send(send_input.at[0], last_input, 4, 6, pass_id).wait_send()
+        send(send_taps, got_taps.at[me], 5, 7, last_id).wait_send()
+        send(send_part, got_part.at[me], 6, 8, last_id).wait_send()
+
+    @pl.when(is_pass)
+    def _():
+        for passed, target, sent, _, received in passes:
+            send(others(passed), others(target), sent, received, last_id).wait_send()
 
 
 def finish(got_back, grad_taps_v, grad_input_hbm, grad_taps_hbm, turned_v, grad_input_v, sem):
@@ -287,7 +454,7 @@
             pltpu.VMEM(block_shape, BF),
             pltpu.VMEM((PENCIL * SIDE, SIDE), F32),
         ),
-        in_specs=[pl.BlockSpec(memory_space=pltpu.HBM)] * 8,
+        in_specs=[pl.BlockSpec(memory_space=pltpu.HBM)] * len(operands),
         out_specs=[pl.BlockSpec(memory_space=pltpu.VMEM)] * 2,
         scratch_shapes=[
             pltpu.VMEM(tile_shape, BF),
@@ -296,11 +463,15 @@
             *[pltpu.VMEM(table.shape, F32 if table.dtype == np.float32 else BF) for table in tables],
             pltpu.VMEM((8, 64, SIDE), F32),
             *[pltpu.VMEM(block_shape, BF)] * 5,
-            pltpu.VMEM((PENCIL * SIDE, 2 * SIDE), F32),
-            pltpu.VMEM((PENCIL * SIDE, 2 * SIDE), F32),
-            pltpu.SemaphoreType.DMA((8,)),
-            pltpu.SemaphoreType.DMA((3,)),
-            pltpu.SemaphoreType.DMA((3,)),
+            *[pltpu.VMEM(block_shape[1:], BF)] * 2,
+            *[pltpu.VMEM(block_shape, BF)] * 2,
+            *[pltpu.VMEM(block_shape[1:], F32)] * 2,
+            *[pltpu.VMEM(block_shape, F32)] * 2,
+            *[pltpu.VMEM((PENCIL * SIDE, 2 * SIDE), F32)] * 2,
+            pltpu.SemaphoreType.DMA((11,)),
+            pltpu.SemaphoreType.DMA((9,)),
+            pltpu.SemaphoreType.DMA((9,)),
+            pltpu.SemaphoreType.REGULAR,
         ],
         compiler_params=pltpu.CompilerParams(
             collective_id=0, has_side_effects=True, vmem_limit_bytes=48 * 1024 * 1024

time: 28.3 us -> 22.3 us (0.79)
  Pallas kernels: 27.5 us -> 21.5 us
    pallas_call x1, Pallas kernels: 26.8 us -> 20.7 us  [shards(): pl.pallas_call(kernel, name='conv_backward', out_shape=(pltpu.VMEM(block_...]
where the time goes in v3:
time: 22.3 us; the launch traced here: 22.1 us
  Pallas kernels  21.5 us (96%)
  between operations  0.64 us (3%)
    pallas_call x1, Pallas kernels, shards(): pl.pallas_call(kernel, name='conv_backward', out_shape=(pltpu.VMEM(block_...  20.7 us
    pallas_call x1, Pallas kernels, shards(): pl.pallas_call(finish, name='conv_backward_finish', out_shape=(jax.ShapeD...  0.76 us

profile of v3, /device:TPU:8, one launch (start us, length us, event | category | flops | bytes accessed | tf_op | source)
XLA Modules:
  0.0 22.1 jit_solution(6015814042523507235)
XLA Ops:
  0.6 20.7 %conv_backward.1 = (bf16[16,4,8,128]{3,2,1,0:T(8,128)(2,1)S(1)}, f32[512,128]{1,0:T(8,128)S(1)}) custom-call(bf16[8,8,8,128]{3,2,1,0:T(8,128)(2,1)} %bitcast.20, bf16[8,8,8,128]{3,2,1,0:T(8,128)(2,1)} %bitcast.21, f32[512,128]{1,0:T(8,128)} %bitcast.19, bf16[256,384]{1,0:T(8,128)(2,1)} %constant.16.clone.first_hbm, f32[2,128,128]{2,1,0:T(8,128)} %constant.17.clone.turns_hbm, ...), custom_call_target="tpu_custom_call" | custom-call | tf_op jit(solution)/shard_map/conv_backward/pallas_call | solution.py:450
  21.4 0.8 %conv_backward_finish.1 = (bf16[8,8,8,128]{3,2,1,0:T(8,128)(2,1)}, f32[512,128]{1,0:T(8,128)}) custom-call(bf16[16,4,8,128]{3,2,1,0:T(8,128)(2,1)S(1)} %get-tuple-element.6.got_back, f32[512,128]{1,0:T(8,128)S(1)} %get-tuple-element.7.grad_taps_v), custom_call_target="tpu_custom_call" | custom-call | tf_op jit(solution)/shard_map/conv_backward_finish/pallas_call | solution.py:480

commit v4 on v3

--- a/solution.py
+++ b/solution.py
@@ -190,6 +190,18 @@
     rows = (row, row + 1 - 2 * (row % 2), (row + 2) % 4, 3 - row)
     peers = [rows[over] * 4 + (column + along) % 4 for over, along in FAR_FIRST]
 
+    barrier = pltpu.get_barrier_semaphore()
+
+    @pl.when(jnp.logical_not(is_last))
+    def _():
+        for peer in peers:
+            pl.semaphore_signal(barrier, inc=1, device_id={"ctx": peer}, device_id_type=MESH)
+
+    @pl.when(is_pass)
+    def _():
+        for peer in range(PEERS):
+            pl.semaphore_signal(barrier, inc=1, device_id={"dp": 0, "ctx": peer}, device_id_type=MESH)
+
     def load(source, target, slot):
         copy = pltpu.make_async_copy(source, target, local_sem.at[slot])
         copy.start()
@@ -215,18 +227,6 @@
         )
     ]
 
-    barrier = pltpu.get_barrier_semaphore()
-
-    @pl.when(jnp.logical_not(is_last))
-    def _():
-        for peer in peers:
-            pl.semaphore_signal(barrier, inc=1, device_id={"ctx": peer}, device_id_type=MESH)
-
-    @pl.when(is_pass)
-    def _():
-        for peer in range(PEERS):
-            pl.semaphore_signal(barrier, inc=1, device_id={"dp": 0, "ctx": peer}, device_id_type=MESH)
-
     def turn_rows(source, target):
         for group in range(8):
             turned_v[group] = source[group].astype(F32).reshape(64, SIDE)
@@ -287,17 +287,17 @@
         def _():
             some_of(source, target, PEERS - 1, slot, slot).wait_recv()
 
+    @pl.when(is_last)
+    def _():
+        pl.semaphore_wait(barrier, PEERS)
+        pl.semaphore_signal(entered_sem, inc=1, device_id=pass_id, device_id_type=MESH)
+
     grad_load.wait()
     turn_rows(grad_v, send_grad)
 
     @pl.when(jnp.logical_not(is_last))
     def _():
         pl.semaphore_wait(barrier, PEERS - 1)
-
-    @pl.when(is_last)
-    def _():
-        pl.semaphore_wait(barrier, PEERS)
-        pl.semaphore_signal(entered_sem, inc=1, device_id=pass_id, device_id_type=MESH)
 
     gather(send_grad, got_grad, 0, last_grad, pass_grad)
     input_load.wait()
@@ -308,7 +308,7 @@
     for channel in range(PENCIL):
         send_taps[channel] = taps_v[pl.ds(channel, BLOCKS, stride=PENCIL), :]
 
-    for copy in table_loads:
+    for copy in table_loads[:3]:
         copy.wait()
 
     taps_spec[...] = forward_wide(
@@ -317,6 +317,9 @@
         turns_v,
         second_v,
     )
+
+    for copy in table_loads[3:5]:
+        copy.wait()
 
     def channels(source):
         return [source[:, channel].reshape(SIDE, SIDE) for channel in range(PENCIL)]
@@ -337,17 +340,20 @@
         send_back[:, channel] = block.astype(BF).reshape(PEERS, BLOCKS, SIDE)
     exchange(send_back, got_back, 2)
 
+    for copy in table_loads[5:]:
+        copy.wait()
+
     all_received(send_input, got_input, 1)
 
     @pl.when(is_ahead)
     def _():
         send(send_grad.at[0], last_grad, 0, 3, last_id).wait_recv()
-        send(send_input.at[0], last_input, 1, 4, last_id).wait_recv()
         send(send_taps, got_taps.at[me], 5, 7, last_id).start()
         send(send_part, got_part.at[me], 6, 8, last_id).start()
         got_grad[0] = last_grad[...]
+        grad_spec[...] = forward(channels(got_grad), first_v, turns_v, second_v)
+        send(send_input.at[0], last_input, 1, 4, last_id).wait_recv()
         got_input[0] = last_input[...]
-        grad_spec[...] = forward(channels(got_grad), first_v, turns_v, second_v)
 
     input_spec = forward(channels(got_input), first_v, turns_v, second_v)
     lags = inverse(

time: 22.3 us -> 21.8 us (0.978)
  Pallas kernels: 21.5 us -> 21 us
    pallas_call x1, Pallas kernels: 20.7 us -> 20.2 us  [shards(): pl.pallas_call(kernel, name='conv_backward', out_shape=(pltpu.VMEM(block_...]
where the time goes in v4:
time: 21.8 us; the launch traced here: 21.6 us
  Pallas kernels  21 us (96%)
  between operations  0.64 us (3%)
    pallas_call x1, Pallas kernels, shards(): pl.pallas_call(kernel, name='conv_backward', out_shape=(pltpu.VMEM(block_...  20.2 us
    pallas_call x1, Pallas kernels, shards(): pl.pallas_call(finish, name='conv_backward_finish', out_shape=(jax.ShapeD...  0.76 us

profile of v4, /device:TPU:8, one launch (start us, length us, event | category | flops | bytes accessed | tf_op | source)
XLA Modules:
  0.0 21.6 jit_solution(11524442468065814723)
XLA Ops:
  0.6 20.2 %conv_backward.1 = (bf16[16,4,8,128]{3,2,1,0:T(8,128)(2,1)S(1)}, f32[512,128]{1,0:T(8,128)S(1)}) custom-call(bf16[8,8,8,128]{3,2,1,0:T(8,128)(2,1)} %bitcast.20, bf16[8,8,8,128]{3,2,1,0:T(8,128)(2,1)} %bitcast.21, f32[512,128]{1,0:T(8,128)} %bitcast.19, bf16[256,384]{1,0:T(8,128)(2,1)} %constant.16.clone.first_hbm, f32[2,128,128]{2,1,0:T(8,128)} %constant.17.clone.turns_hbm, ...), custom_call_target="tpu_custom_call" | custom-call | tf_op jit(solution)/shard_map/conv_backward/pallas_call | solution.py:456
  20.9 0.8 %conv_backward_finish.1 = (bf16[8,8,8,128]{3,2,1,0:T(8,128)(2,1)}, f32[512,128]{1,0:T(8,128)}) custom-call(bf16[16,4,8,128]{3,2,1,0:T(8,128)(2,1)S(1)} %get-tuple-element.6.got_back, f32[512,128]{1,0:T(8,128)S(1)} %get-tuple-element.7.grad_taps_v), custom_call_target="tpu_custom_call" | custom-call | tf_op jit(solution)/shard_map/conv_backward_finish/pallas_call | solution.py:486

commit v5 on v4

--- a/solution.py
+++ b/solution.py
@@ -23,6 +23,16 @@
 )
 
 
+def wide_rows(table_v):
+    half = table_v.shape[0] // 2
+    return jnp.concatenate([table_v[:half], table_v[:half], table_v[half:]], axis=0)
+
+
+def wide_columns(table_v):
+    half = table_v.shape[0] // 2
+    return jnp.concatenate([table_v[:half], table_v[:half], table_v[half:]], axis=1)
+
+
 def split_table(values):
     high = values.astype(ml_dtypes.bfloat16)
     low = (values - high.astype(np.float64)).astype(ml_dtypes.bfloat16)
@@ -34,37 +44,37 @@
     index = np.arange(SIDE, dtype=np.int64)
     first = ((4 * index[:, None] + 1) * index[None, :]) % (4 * SIDE) * (2.0 * np.pi / (4 * SIDE))
     first_high, first_low = split_table(np.concatenate([np.cos(first), -np.sin(first)], axis=0))
-    forward_first = np.concatenate([first_high, first_low, first_high], axis=1)
+    forward_first = np.concatenate([first_high, first_low], axis=1)
     turn = ((4 * index[:, None] + 1) * index[None, :]) % (4 * total) * (2.0 * np.pi / (4 * total))
     turns = np.stack([np.cos(turn), np.sin(turn)]).astype(np.float32)
     second = (index[:, None] * index[None, :]) % SIDE * (2.0 * np.pi / SIDE)
     cos_two, sin_two = np.cos(second), np.sin(second)
     high, low = split_table(np.block([[cos_two, -sin_two], [sin_two, cos_two]]))
-    forward_second = np.concatenate([high, high, low], axis=0)
+    forward_second = np.concatenate([high, low], axis=0)
     high, low = split_table(np.block([[cos_two, sin_two], [-sin_two, cos_two]]))
-    inverse_second = np.concatenate([high, high, low], axis=0)
+    inverse_second = np.concatenate([high, low], axis=0)
     high, low = split_table(np.concatenate([np.cos(first).T, -np.sin(first).T], axis=1) / total)
-    inverse_first = np.concatenate([high, high, low], axis=1)
+    inverse_first = np.concatenate([high, low], axis=0)
     short, each = index[:BLOCKS], np.eye(SIDE // BLOCKS)
     first = ((4 * short[:, None] + 1) * short[None, :]) % (4 * BLOCKS) * (2.0 * np.pi / (4 * BLOCKS))
     real, imag = np.kron(each, np.cos(first)), np.kron(each, -np.sin(first))
     high, low = split_table(np.concatenate([real, imag], axis=0))
-    local_first = np.concatenate([high, low, high], axis=1)
+    local_first = np.concatenate([high, low], axis=1)
     high, low = split_table(np.concatenate([real.T, imag.T], axis=1) / (BLOCKS * SIDE))
-    local_inverse_first = np.concatenate([high, high, low], axis=1)
+    local_inverse_first = np.concatenate([high, low], axis=0)
     turn = (4 * short[:, None] + 1) * index[None, :] * (2.0 * np.pi / (4 * BLOCKS * SIDE))
     turn = np.tile(turn, (SIDE // BLOCKS, 1))
     local_turns = np.stack([np.cos(turn), np.sin(turn)]).astype(np.float32)
-    return (
-        forward_first,
-        turns,
-        forward_second,
-        inverse_second,
-        inverse_first,
-        local_first,
-        local_turns,
-        local_inverse_first,
-    )
+    parts = (forward_first, forward_second, inverse_second, inverse_first, local_first, local_inverse_first)
+    return np.concatenate(parts, axis=0), np.concatenate([turns, local_turns], axis=0)
+
+
+def table_views(tables_v, turns_v):
+    views, start = [], 0
+    for count in (2 * SIDE, 4 * SIDE, 4 * SIDE, 2 * SIDE, 2 * SIDE, 2 * SIDE):
+        views.append(tables_v.at[start : start + count])
+        start += count
+    return views, turns_v.at[:2], turns_v.at[2:]
 
 
 def halves(value):
@@ -97,17 +107,17 @@
         real = first[:SIDE, at * SIDE : (at + 1) * SIDE]
         imag = first[SIDE:, at * SIDE : (at + 1) * SIDE]
         pairs.append((real * cos_turn + imag * sin_turn, imag * cos_turn - real * sin_turn))
-    return jnp.dot(stacked_rows(pairs, False), second_v[...], preferred_element_type=F32)
+    return jnp.dot(stacked_rows(pairs, False), wide_rows(second_v), preferred_element_type=F32)
 
 
 def inverse(pairs, turns_v, inverse_second_v, inverse_first_v):
-    mixed = jnp.dot(stacked_rows(pairs, False), inverse_second_v[...], preferred_element_type=F32)
+    mixed = jnp.dot(stacked_rows(pairs, False), wide_rows(inverse_second_v), preferred_element_type=F32)
     cos_turn, sin_turn = turns_v[0], turns_v[1]
     turned = [
         (real * cos_turn - imag * sin_turn, imag * cos_turn + real * sin_turn)
         for real, imag in channel_parts(mixed)
     ]
-    return jnp.dot(inverse_first_v[...], stacked_rows(turned, True), preferred_element_type=F32)
+    return jnp.dot(wide_columns(inverse_first_v), stacked_rows(turned, True), preferred_element_type=F32)
 
 
 def forward_wide(blocks, first_v, turns_v, second_v):
@@ -115,14 +125,15 @@
     for block in blocks:
         high, low = halves(block)
         columns.append(jnp.concatenate([high, high, low], axis=0))
-    first = jnp.dot(first_v[...], jnp.concatenate(columns, axis=1), preferred_element_type=F32)
+    table = jnp.concatenate([first_v[...], first_v[:, :SIDE]], axis=1)
+    first = jnp.dot(table, jnp.concatenate(columns, axis=1), preferred_element_type=F32)
     return second_stage(first, turns_v, second_v)
 
 
 def forward(blocks, first_v, turns_v, second_v):
     rows = jnp.concatenate(blocks, axis=1)
     first = jnp.dot(
-        first_v[:, : 2 * SIDE], jnp.concatenate([rows, rows], axis=0), preferred_element_type=F32
+        first_v[...], jnp.concatenate([rows, rows], axis=0), preferred_element_type=F32
     )
     return second_stage(first, turns_v, second_v)
 
@@ -138,27 +149,15 @@
     grad_hbm,
     input_hbm,
     taps_hbm,
-    first_hbm,
+    tables_hbm,
     turns_hbm,
-    second_hbm,
-    inverse_second_hbm,
-    inverse_first_hbm,
-    local_first_hbm,
-    local_turns_hbm,
-    local_inverse_first_hbm,
     got_back,
     grad_taps_v,
     grad_v,
     input_v,
     taps_v,
-    first_v,
-    turns_v,
-    second_v,
-    inverse_second_v,
-    inverse_first_v,
-    local_first_v,
-    local_turns_v,
-    local_inverse_first_v,
+    tables_v,
+    all_turns_v,
     turned_v,
     send_grad,
     send_input,
@@ -210,22 +209,9 @@
     grad_load = load(grad_hbm, grad_v, 0)
     input_load = load(input_hbm, input_v, 1)
     taps_load = load(taps_hbm, taps_v, 2)
-    table_loads = [
-        load(source, target, slot)
-        for slot, (source, target) in enumerate(
-            (
-                (first_hbm, first_v),
-                (turns_hbm, turns_v),
-                (second_hbm, second_v),
-                (inverse_second_hbm, inverse_second_v),
-                (inverse_first_hbm, inverse_first_v),
-                (local_first_hbm, local_first_v),
-                (local_turns_hbm, local_turns_v),
-                (local_inverse_first_hbm, local_inverse_first_v),
-            ),
-            3,
-        )
-    ]
+    table_loads = [load(tables_hbm, tables_v, 3), load(turns_hbm, all_turns_v, 4)]
+    views, turns_v, local_turns_v = table_views(tables_v, all_turns_v)
+    first_v, second_v, inverse_second_v, inverse_first_v, local_first_v, local_inverse_first_v = views
 
     def turn_rows(source, target):
         for group in range(8):
@@ -304,11 +290,16 @@
     turn_rows(input_v, send_input)
     gather(send_input, got_input, 1, last_input, pass_input)
 
+    @pl.when(is_last)
+    def _():
+        for peer in peers:
+            pl.semaphore_signal(entered_sem, inc=1, device_id={"ctx": peer}, device_id_type=MESH)
+
     taps_load.wait()
     for channel in range(PENCIL):
         send_taps[channel] = taps_v[pl.ds(channel, BLOCKS, stride=PENCIL), :]
 
-    for copy in table_loads[:3]:
+    for copy in table_loads:
         copy.wait()
 
     taps_spec[...] = forward_wide(
@@ -317,9 +308,6 @@
         turns_v,
         second_v,
     )
-
-    for copy in table_loads[3:5]:
-        copy.wait()
 
     def channels(source):
         return [source[:, channel].reshape(SIDE, SIDE) for channel in range(PENCIL)]
@@ -338,18 +326,27 @@
         block = back[:, channel * SIDE : (channel + 1) * SIDE]
         send_part[channel] = block[:BLOCKS]
         send_back[:, channel] = block.astype(BF).reshape(PEERS, BLOCKS, SIDE)
-    exchange(send_back, got_back, 2)
-
-    for copy in table_loads[5:]:
-        copy.wait()
+
+    @pl.when(is_last)
+    def _():
+        for peer in reversed(peers):
+            send(send_back.at[peer], got_back.at[me], 2, 2, {"ctx": peer}).start()
+
+        got_back[me] = send_back[me]
+
+    @pl.when(jnp.logical_not(is_last))
+    def _():
+        exchange(send_back, got_back, 2)
+
 
     all_received(send_input, got_input, 1)
 
     @pl.when(is_ahead)
     def _():
-        send(send_grad.at[0], last_grad, 0, 3, last_id).wait_recv()
+        pl.semaphore_wait(entered_sem, 1)
         send(send_taps, got_taps.at[me], 5, 7, last_id).start()
         send(send_part, got_part.at[me], 6, 8, last_id).start()
+        send(send_grad.at[0], last_grad, 0, 3, last_id).wait_recv()
         got_grad[0] = last_grad[...]
         grad_spec[...] = forward(channels(got_grad), first_v, turns_v, second_v)
         send(send_input.at[0], last_input, 1, 4, last_id).wait_recv()
@@ -474,7 +471,7 @@
             *[pltpu.VMEM(block_shape[1:], F32)] * 2,
             *[pltpu.VMEM(block_shape, F32)] * 2,
             *[pltpu.VMEM((PENCIL * SIDE, 2 * SIDE), F32)] * 2,
-            pltpu.SemaphoreType.DMA((11,)),
+            pltpu.SemaphoreType.DMA((5,)),
             pltpu.SemaphoreType.DMA((9,)),
             pltpu.SemaphoreType.DMA((9,)),
             pltpu.SemaphoreType.REGULAR,

time: 21.8 us -> 21.7 us (level)
  no operation moved by 1% of the time
where the time goes in v5:
time: 21.7 us; the launch traced here: 21.5 us
  Pallas kernels  20.9 us (96%)
  between operations  0.64 us (3%)
    pallas_call x1, Pallas kernels, shards(): pl.pallas_call(kernel, name='conv_backward', out_shape=(pltpu.VMEM(block_...  20.1 us
    pallas_call x1, Pallas kernels, shards(): pl.pallas_call(finish, name='conv_backward_finish', out_shape=(jax.ShapeD...  0.76 us

profile of v5, /device:TPU:8, one launch (start us, length us, event | category | flops | bytes accessed | tf_op | source)
XLA Modules:
  0.0 21.5 jit_solution(8715116032500180508)
XLA Ops:
  0.6 20.1 %conv_backward.1 = (bf16[16,4,8,128]{3,2,1,0:T(8,128)(2,1)S(1)}, f32[512,128]{1,0:T(8,128)S(1)}) custom-call(bf16[8,8,8,128]{3,2,1,0:T(8,128)(2,1)} %bitcast.20, bf16[8,8,8,128]{3,2,1,0:T(8,128)(2,1)} %bitcast.21, f32[512,128]{1,0:T(8,128)} %bitcast.19, bf16[2048,256]{1,0:T(8,128)(2,1)} %constant.4.clone.tables_hbm, f32[4,128,128]{2,1,0:T(8,128)} %constant.5.clone.turns_hbm), custom_call_target="tpu_custom_call" | custom-call | tf_op jit(solution)/shard_map/conv_backward/pallas_call | solution.py:453
  20.7 0.8 %conv_backward_finish.1 = (bf16[8,8,8,128]{3,2,1,0:T(8,128)(2,1)}, f32[512,128]{1,0:T(8,128)}) custom-call(bf16[16,4,8,128]{3,2,1,0:T(8,128)(2,1)S(1)} %get-tuple-element.6.got_back, f32[512,128]{1,0:T(8,128)S(1)} %get-tuple-element.7.grad_taps_v), custom_call_target="tpu_custom_call" | custom-call | tf_op jit(solution)/shard_map/conv_backward_finish/pallas_call | solution.py:483
